TPU v7x, 32 devices: a whole 2x2x4 slice. The times are simulated.
32 devices in a mesh: row: 4 (over z), col: 8 (over y, x, core).
Axes of the slice: x: 2, y: 2, z: 4, core: 2. Of those that a mesh axis runs over, the one named last changes fastest.
Arguments:
- base_flat: bfloat16 [2, 29568, 8192], P(None, ('row', 'col')), may hold values from -6 to 6
- adjusted_flat: bfloat16 [2, 29568, 8192], P(None, ('row', 'col')), may hold values from -6 to 6
- omega: bfloat16 [2, 8192, 256], P(None, 'col'), may hold values from -6 to 6
Outputs:
- adapter_up_basis: float32 [2, 29568, 256], P(None, ('row', 'col'))
- adapter_down_transposed: float32 [2, 8192, 256], P(None, 'col', 'row')
All inputs are finite; a program needn't handle non-finite values.
Results may differ from a plain program's by a relative error of at most 0.011.
Values may be sent and summed in bfloat16 or wider, within the bound.
No kernel may reach another device: no remote copies, remote signals or barrier semaphores. Data moves between devices by JAX's collectives and lax.ppermute only.
A program may use at most 192 MiB of HBM per device.

v0:
```python
import math
import jax
import jax.numpy as jnp
from jax import lax
from jax.sharding import PartitionSpec as P

HIDDEN_UNITS = 29568


def sketch_term(blocks, right):
    terms = []
    for index in range(blocks.shape[0]):
        rows = blocks[index]
        terms.append(jnp.dot(rows, right[index], preferred_element_type=jnp.float32))
    return jnp.concatenate(terms, axis=1)


def gram_of(panel, matrix_list, adapter_rank):
    panel_three = panel.reshape(panel.shape[0], matrix_list, adapter_rank)
    return jnp.einsum("rmk,rml->mkl", panel_three, panel_three, precision=lax.Precision.HIGHEST)


def orthonormal(panel, gram_total, matrix_list, adapter_rank):
    lower = jnp.linalg.cholesky(gram_total)
    stacked = panel.reshape(panel.shape[0], matrix_list, adapter_rank).transpose(1, 2, 0)
    solved = jax.scipy.linalg.solve_triangular(lower, stacked, lower=True)
    return solved.transpose(2, 0, 1).reshape(panel.shape[0], matrix_list * adapter_rank)


def contract(total, blocks, piece):
    adapter_rank = total.shape[2]
    terms = []
    for index in range(blocks.shape[0]):
        rows = blocks[index]
        terms.append(
            lax.dot_general(
                rows,
                piece[:, index * adapter_rank : (index + 1) * adapter_rank],
                (((0,), (0,)), ((), ())),
                preferred_element_type=jnp.float32,
            )
        )
    return jnp.stack(terms)


def local(base_flat, adjusted_flat, omega):
    matrix_list = base_flat.shape[0]
    adapter_rank = omega.shape[2]
    delta = (adjusted_flat.astype(jnp.float32) - base_flat.astype(jnp.float32)).astype(jnp.bfloat16)
    blocks = lax.all_to_all(delta, "col", split_axis=2, concat_axis=1, tiled=True)
    block_rows = blocks.shape[1]
    block_cols = blocks.shape[2]
    segment_rows = block_rows // lax.axis_size("col")
    col_index = lax.axis_index("col")
    empty = jnp.zeros((matrix_list, block_cols, adapter_rank), jnp.float32)

    def find_basis(right):
        panel = lax.psum(sketch_term(blocks, right), "col")
        gram_total = lax.psum(gram_of(panel, matrix_list, adapter_rank), "row")
        basis = orthonormal(panel, gram_total, matrix_list, adapter_rank)
        own_rows = lax.dynamic_slice_in_dim(basis, col_index * segment_rows, segment_rows, 0)
        folded = contract(empty, blocks, basis.astype(jnp.bfloat16))
        return (own_rows, folded)

    first_rows, first_folded = find_basis(omega)
    shares = lax.psum_scatter(first_folded, "row", scatter_dimension=1, tiled=True)
    columns = lax.all_gather(shares.astype(jnp.bfloat16), "row", axis=1, tiled=True)
    last_basis_rows, last_folded_rows = find_basis(columns)
    adapter_down_transposed = lax.psum_scatter(
        last_folded_rows.astype(jnp.bfloat16), "row", scatter_dimension=2, tiled=True
    ).astype(jnp.float32)
    adapter_up_basis = (
        (math.sqrt(HIDDEN_UNITS) * last_basis_rows)
        .reshape(segment_rows, matrix_list, adapter_rank)
        .transpose(1, 0, 2)
    )
    return (adapter_up_basis, adapter_down_transposed)


def solution(mesh):
    in_specs = (P(None, ("row", "col"), None), P(None, ("row", "col"), None), P(None, "col", None))
    out_specs = (P(None, ("row", "col"), None), P(None, "col", "row"))
    return jax.shard_map(local, mesh=mesh, in_specs=in_specs, out_specs=out_specs, check_vma=False)
```

profile of v0, /device:TPU:0, one launch (start us, length us, event | category | flops | bytes accessed | tf_op | source)
XLA Modules:
  0.0 1735.4 jit_solution(16130789027910597710)
XLA Ops:
  7.2 31.4 %subtract_convert_fusion = bf16[2,924,8192]{2,1,0:T(8,128)(2,1)} fusion(bf16[2,924,8192]{2,0,1:T(2,128)(2,1)} %param.6, bf16[2,924,8192]{2,0,1:T(2,128)(2,1)} %param.7), kind=kLoop, calls=%fused_computation.4 | loop fusion | flops 60555264 | bytes 90832896 | tf_op jit(solution)/shard_map/convert_element_type | solution.py:49
  38.6 82.0 %copy.117 = bf16[2,924,8192]{1,0,2:T(2,128)(2,1)} copy(bf16[2,924,8192]{2,1,0:T(8,128)(2,1)} %subtract_convert_fusion) | data formatting | bytes 60555264 | tf_op jit(solution)/shard_map/convert_element_type | solution.py:49
  120.7 375.5 %all_to_all.15 = bf16[2,924,8192]{1,0,2:T(2,128)(2,1)} all-to-all(bf16[2,924,8192]{1,0,2:T(2,128)(2,1)} %copy.117), channel_id=1, replica_groups=mesh['row'=4,'col'=8] {'col'}, dimensions={2} | all-to-all | bytes 60555264 | tf_op jit(solution)/shard_map/all_to_all | solution.py:50
  496.2 80.7 %copy.118 = bf16[2,924,8,1024]{3,1,2,0:T(8,128)(2,1)} copy(bf16[2,924,8,1024]{1,0,3,2:T(2,128)(2,1)} %bitcast.130) | data formatting | bytes 60555264 | tf_op jit(solution)/shard_map/all_to_all | solution.py:50
  576.9 21.5 %fusion.53 = (bf16[1,8,924,1024]{3,2,1,0:T(8,128)(2,1)}, bf16[1,8,924,1024]{3,2,1,0:T(8,128)(2,1)}) fusion(bf16[2,8,924,1024]{3,2,1,0:T(8,128)(2,1)} %bitcast.131), kind=kLoop, calls=%fused_computation.89 | loop fusion | bytes 60555264 | tf_op jit(solution)/shard_map/slice | solution.py:13
  598.3 11.5 squeeze.26
  609.8 11.6 squeeze.24
  621.4 7.8 fusion.35
  631.0 6.5 fusion.37
  637.5 9.5 pad_maximum_fusion
  647.1 11.8 copy.165
  658.9 200.5 %all-reduce.8.cloned.1.call-done = f32[7392,2,256]{2,0,1:T(8,128)} async-done(((f32[7392,2,256]{2,0,1:T(8,128)}), f32[7392,2,256]{2,0,1:T(8,128)}) %all-reduce.8.cloned.1.call-update) | async-done | bytes 15138832 | tf_op jit(solution)/shard_map/psum | solution.py:58
  859.5 31.0 %fusion.54 = f32[2,256,256]{1,2,0:T(8,128)} fusion(f32[7392,2,256]{2,0,1:T(8,128)} %all-reduce.8.cloned.1.call-done), kind=kOutput, calls=%fused_computation.90 | convolution fusion | flops 11626610688 | bytes 15663104 | tf_op jit(solution)/shard_map/rmk,rml->mkl/dot_general | solution.py:20
  890.6 38.5 %all-reduce.10.cloned.1.call-done = f32[2,256,256]{1,2,0:T(8,128)} async-done(((f32[2,256,256]{1,2,0:T(8,128)}), f32[2,256,256]{1,2,0:T(8,128)}) %all-reduce.10.cloned.1.call-update) | async-done | bytes 524304 | tf_op jit(solution)/shard_map/psum | solution.py:59
  931.5 23.5 %custom-call.17 = f32[2,128,128]{2,1,0:T(8,128)S(1)} custom-call(f32[2,128,128]{2,1,0:T(8,128)S(1)} %cholesky.198), custom_call_target="Cholesky" | custom-call | tf_op jit(solution)/shard_map/jit(cholesky)/cholesky | solution.py:24
  955.0 19.7 %custom-call.18 = f32[2,1,128,128]{2,3,1,0:T(8,128)S(1)} custom-call(f32[2,1,128,128]{3,2,1,0:T(8,128)S(1)} %select_bitcast_fusion.1), custom_call_target="InvertDiagBlocksLowerTriangular" | custom-call | tf_op jit(solution)/shard_map/jit(cholesky)/cholesky | solution.py:24
  975.4 23.5 %custom-call.19 = f32[2,128,128]{2,1,0:T(8,128)S(1)} custom-call(f32[2,128,128]{2,1,0:T(8,128)S(1)} %convolution_subtract_fusion.3), custom_call_target="Cholesky" | custom-call | tf_op jit(solution)/shard_map/jit(cholesky)/cholesky | solution.py:24
  999.3 4.0 while.4
  1003.3 39.3 %custom-call.20 = f32[2,2,128,128]{2,3,1,0:T(8,128)S(1)} custom-call(f32[2,2,128,128]{3,2,1,0:T(8,128)S(1)} %bitcast.144), custom_call_target="InvertDiagBlocksLowerTriangular" | custom-call | tf_op jit(solution)/shard_map/jit(_solve_triangular)/vmap()/triangular_solve | solution.py:26
  1042.6 8.9 fusion.3
  1051.5 6.7 convolution_subtract_fusion.1
  1058.2 7.5 fusion.46
  1065.7 8.3 fusion
  1074.0 10.2 copy.127
  1084.2 8.9 fusion.13
  1097.2 4.1 fusion.16
  1102.9 43.5 %reduce-scatter.2.cloned.1.call-done = f32[2,256,256]{2,1,0:T(8,128)} async-done(((f32[2,1024,256]{2,1,0:T(8,128)}), f32[2,256,256]{2,1,0:T(8,128)}) %reduce-scatter.2.cloned.1.call-update) | async-done | bytes 524304 | tf_op jit(solution)/shard_map/reduce_scatter | solution.py:66
  1148.2 27.4 %all-gather.2.cloned.1.call-done = bf16[2,1024,256]{2,1,0:T(8,128)(2,1)} async-done(((bf16[2,256,256]{2,1,0:T(8,128)(2,1)}), bf16[2,1024,256]{2,1,0:T(8,128)(2,1)}) %all-gather.2.cloned.1.call-update) | async-done | bytes 1048592 | tf_op jit(solution)/shard_map/all_gather | solution.py:67
  1175.6 9.8 fusion.32
  1185.4 7.6 fusion.31
  1193.1 5.9 pad_maximum_fusion.1
  1199.0 11.8 copy.164
  1210.8 199.8 %all-reduce.12.cloned.1.call-done = f32[7392,2,256]{2,0,1:T(8,128)} async-done(((f32[7392,2,256]{2,0,1:T(8,128)}), f32[7392,2,256]{2,0,1:T(8,128)}) %all-reduce.12.cloned.1.call-update) | async-done | bytes 15138832 | tf_op jit(solution)/shard_map/psum | solution.py:58
  1410.7 30.9 %fusion.55 = f32[2,256,256]{1,2,0:T(8,128)} fusion(f32[7392,2,256]{2,0,1:T(8,128)} %all-reduce.12.cloned.1.call-done), kind=kOutput, calls=%fused_computation.91 | convolution fusion | flops 11626610688 | bytes 15663104 | tf_op jit(solution)/shard_map/rmk,rml->mkl/dot_general | solution.py:20
  1441.7 38.6 %all-reduce.14.cloned.1.call-done = f32[2,256,256]{1,2,0:T(8,128)} async-done(((f32[2,256,256]{1,2,0:T(8,128)}), f32[2,256,256]{1,2,0:T(8,128)}) %all-reduce.14.cloned.1.call-update) | async-done | bytes 524304 | tf_op jit(solution)/shard_map/psum | solution.py:59
  1482.7 23.5 %custom-call.21 = f32[2,128,128]{2,1,0:T(8,128)S(1)} custom-call(f32[2,128,128]{2,1,0:T(8,128)S(1)} %cholesky.201), custom_call_target="Cholesky" | custom-call | tf_op jit(solution)/shard_map/jit(cholesky)/cholesky | solution.py:24
  1506.2 19.7 %custom-call.22 = f32[2,1,128,128]{2,3,1,0:T(8,128)S(1)} custom-call(f32[2,1,128,128]{3,2,1,0:T(8,128)S(1)} %select_bitcast_fusion), custom_call_target="InvertDiagBlocksLowerTriangular" | custom-call | tf_op jit(solution)/shard_map/jit(cholesky)/cholesky | solution.py:24
  1526.5 23.5 %custom-call.23 = f32[2,128,128]{2,1,0:T(8,128)S(1)} custom-call(f32[2,128,128]{2,1,0:T(8,128)S(1)} %convolution_subtract_fusion.2), custom_call_target="Cholesky" | custom-call | tf_op jit(solution)/shard_map/jit(cholesky)/cholesky | solution.py:24
  1554.5 39.3 %custom-call.24 = f32[2,2,128,128]{2,3,1,0:T(8,128)S(1)} custom-call(f32[2,2,128,128]{3,2,1,0:T(8,128)S(1)} %bitcast.143), custom_call_target="InvertDiagBlocksLowerTriangular" | custom-call | tf_op jit(solution)/shard_map/jit(_solve_triangular)/vmap()/triangular_solve | solution.py:26
  1593.8 8.9 fusion.1
  1602.7 6.7 convolution_subtract_fusion
  1609.4 8.1 fusion.42
  1617.5 11.5 maximum_bitcast_fusion
  1629.0 15.4 copy.136
  1644.4 9.2 bitcast_convert_fusion
  1653.6 10.7 fusion.28
  1664.3 7.8 fusion.25
  1680.2 46.0 %all-reduce.16.cloned.1.call-done = bf16[2,1024,256]{1,0,2:T(2,128)(2,1)} async-done(((bf16[2,1024,256]{1,0,2:T(2,128)(2,1)}), bf16[2,1024,256]{1,0,2:T(2,128)(2,1)}) %all-reduce.16.cloned.1.call-update) | async-done | bytes 1048592
  (95 shorter events, 37.9 us)
Async XLA Ops:
  7.2 852.3 %all-reduce.8.cloned.1.call-start = ((), (), s32[]{:S(2)}) async-start(), calls=%async_computation.2 | async-start | bytes 30277632 | tf_op jit(solution)/shard_map/psum | solution.py:58
  609.8 11.6 copy-start.7
  621.4 9.6 copy-start.4
  658.9 270.3 %all-reduce.10.cloned.1.call-start = ((), (), s32[]{:S(2)}) async-start(), calls=%async_computation.3 | async-start | bytes 1048576 | tf_op jit(solution)/shard_map/psum | solution.py:59
  890.5 255.9 %reduce-scatter.2.cloned.1.call-start = ((), (), s32[]{:S(2)}) async-start(), calls=%async_computation.4 | async-start | bytes 2621440 | tf_op jit(solution)/shard_map/reduce_scatter | solution.py:66
  1042.6 8.9 copy-start
  1051.5 6.7 copy-start.2
  1084.2 9.0 slice-start
  1084.2 9.8 copy-start.6
  1084.2 11.0 slice-start.1
  1084.2 12.2 slice-start.2
  1084.2 12.9 slice-start.3
  1102.8 72.8 %all-gather.2.cloned.1.call-start = ((), (), s32[]{:S(2)}) async-start(), calls=%async_computation.5 | async-start | bytes 1310720 | tf_op jit(solution)/shard_map/all_gather | solution.py:67
  1148.2 262.5 %all-reduce.12.cloned.1.call-start = ((), (), s32[]{:S(2)}) async-start(), calls=%async_computation.6 | async-start | bytes 30277632 | tf_op jit(solution)/shard_map/psum | solution.py:58
  1175.6 9.8 copy-start.8
  1210.8 269.5 %all-reduce.14.cloned.1.call-start = ((), (), s32[]{:S(2)}) async-start(), calls=%async_computation.7 | async-start | bytes 1048576 | tf_op jit(solution)/shard_map/psum | solution.py:59
  1441.6 284.7 %all-reduce.16.cloned.1.call-start = ((), (), s32[]{:S(2)}) async-start(), calls=%async_computation.8 | async-start | bytes 2097152
  1593.8 8.9 copy-start.1
  1602.7 6.7 copy-start.3
  1653.6 10.7 copy-start.5
  1664.3 10.2 copy-start.9
Sparse Core Ops, SparseCore 0:
  659.0 200.4 all-reduce.7
  890.6 38.4 all-reduce.9
  1102.9 43.4 reduce-scatter.1
  1148.4 27.1 all-gather.1
  1210.9 199.7 all-reduce.11
  1441.7 38.5 all-reduce.13
  1674.6 51.6 all-reduce.15
where the time goes:
time: 1750 us; the launch traced here: 1740 us
  waiting for transfers between devices  595 us (34%)
  blocking collectives  376 us (21%)
  other arithmetic  298 us (17%)
  local copies, waits for them, and re-layouts  279 us (16%)
  matrix products  173 us (10%)
    psum x2, waiting for transfers between devices, find_basis(): panel = lax.psum(sketch_term(blocks, right), 'col')  400 us
    all_to_all x1, blocking collectives, local(): lax.all_to_all(delta, 'col', split_axis=2, concat_axis=1, tiled=True)  376 us
    another operation x17, other arithmetic, orthonormal(): lower = jnp.linalg.cholesky(gram_total)  134 us
    convert_element_type x1, local copies, waits for them, and re-layouts, local(): (adjusted_flat.astype(jnp.float32) - base_flat.astype(jnp.float32)).astyp...  82 us
    all_to_all x1, local copies, waits for them, and re-layouts, local(): lax.all_to_all(delta, 'col', split_axis=2, concat_axis=1, tiled=True)  80.7 us
    another operation x6, other arithmetic, orthonormal(): solved = jax.scipy.linalg.solve_triangular(lower, stacked, lower=True)  79 us
    psum x2, waiting for transfers between devices, find_basis(): gram_total = lax.psum(gram_of(panel, matrix_list, adapter_rank), 'row')  77.2 us
    dot_general x2, matrix products, gram_of(): jnp.einsum('rmk,rml->mkl', panel_three, panel_three, precision=lax.Precis...  61.9 us
  transfers between devices with their start and end apart: 7, of which 7 were waited for; matrix products, arithmetic and copies ran while one was open for 0% of the time, Pallas kernels for 0%

commit v1 on v0

--- a/solution.py
+++ b/solution.py
@@ -47,7 +47,10 @@
     matrix_list = base_flat.shape[0]
     adapter_rank = omega.shape[2]
     delta = (adjusted_flat.astype(jnp.float32) - base_flat.astype(jnp.float32)).astype(jnp.bfloat16)
-    blocks = lax.all_to_all(delta, "col", split_axis=2, concat_axis=1, tiled=True)
+    blocks = jnp.concatenate(
+        lax.all_to_all(jnp.stack(jnp.split(delta, lax.axis_size("col"), axis=2)), "col", 0, 0),
+        axis=1,
+    )
     block_rows = blocks.shape[1]
     block_cols = blocks.shape[2]
     segment_rows = block_rows // lax.axis_size("col")

time: 1750 us -> 2160 us (1.23)
  local copies, waits for them, and re-layouts: 279 us -> 721 us
  blocking collectives: 376 us -> 340 us
    slice x1 -> x2, local copies, waits for them, and re-layouts: 21.5 us -> 574 us  [sketch_term(): rows = blocks[index]]
    convert_element_type x1 -> x0, local copies, waits for them, and re-layouts: 82 us -> none  [local(): (adjusted_flat.astype(jnp.float32) - base_flat.astype(jnp.float32)).astyp...]
    all_to_all x1 -> x0, local copies, waits for them, and re-layouts: 80.7 us -> none  [local(): lax.all_to_all(delta, 'col', split_axis=2, concat_axis=1, tiled=True)]
    unnamed x30 -> x37, local copies, waits for them, and re-layouts: 7.39 us -> 53.4 us
    all_to_all x1, blocking collectives: 376 us -> 340 us  [local(): lax.all_to_all(jnp.stack(jnp.split(delta, lax.axis_size('col'), axis=2)),...]
where the time goes in v1:
time: 2160 us; the launch traced here: 2150 us
  local copies, waits for them, and re-layouts  721 us (33%)
  waiting for transfers between devices  595 us (28%)
  blocking collectives  340 us (16%)
  other arithmetic  306 us (14%)
  matrix products  173 us (8%)
    slice x2, local copies, waits for them, and re-layouts, sketch_term(): rows = blocks[index]  574 us
    psum x2, waiting for transfers between devices, find_basis(): panel = lax.psum(sketch_term(blocks, right), 'col')  400 us
    all_to_all x1, blocking collectives, local(): lax.all_to_all(jnp.stack(jnp.split(delta, lax.axis_size('col'), axis=2)),...  340 us
    another operation x17, other arithmetic, orthonormal(): lower = jnp.linalg.cholesky(gram_total)  134 us
    another operation x6, other arithmetic, orthonormal(): solved = jax.scipy.linalg.solve_triangular(lower, stacked, lower=True)  79 us
    psum x2, waiting for transfers between devices, find_basis(): gram_total = lax.psum(gram_of(panel, matrix_list, adapter_rank), 'row')  77.2 us
    dot_general x2, matrix products, gram_of(): jnp.einsum('rmk,rml->mkl', panel_three, panel_three, precision=lax.Precis...  61.9 us
    unnamed x37, local copies, waits for them, and re-layouts  53.4 us
  transfers between devices with their start and end apart: 7, of which 7 were waited for; matrix products, arithmetic and copies ran while one was open for 0% of the time, Pallas kernels for 0%

profile of v1, /device:TPU:0, one launch (start us, length us, event | category | flops | bytes accessed | tf_op | source)
XLA Modules:
  0.0 2150.3 jit_solution(13536002849445281)
XLA Ops:
  7.2 39.5 %subtract_convert_fusion = bf16[2,924,8192]{2,0,1:T(2,128)(2,1)} fusion(bf16[2,924,8192]{2,0,1:T(2,128)(2,1)} %param.6, bf16[2,924,8192]{2,0,1:T(2,128)(2,1)} %param.7), kind=kLoop, calls=%fused_computation.4 | loop fusion | flops 60555264 | bytes 90832896 | tf_op jit(solution)/shard_map/convert_element_type | solution.py:49
  46.7 6.5 fusion.20
  53.2 6.6 fusion.19
  66.3 6.5 fusion.17
  72.8 7.0 fusion.16
  92.8 6.5 fusion.13
  99.3 339.8 %all_to_all.5 = bf16[8,2,924,1024]{3,1,2,0:T(2,128)(2,1)} all-to-all(bf16[8,2,924,1024]{3,1,2,0:T(2,128)(2,1)} %fusion.13), channel_id=1, replica_groups=mesh['row'=4,'col'=8] {'col'}, dimensions={0} | all-to-all | bytes 60555264 | tf_op jit(solution)/shard_map/all_to_all | solution.py:51
  439.1 268.8 %slice_reduce_fusion = bf16[8,924,1024]{2,1,0:T(8,128)(2,1)} fusion(bf16[2,8,924,1024]{3,0,2,1:T(2,128)(2,1)} %bitcast.157), kind=kLoop, calls=%fused_computation.5 | loop fusion | bytes 30277632 | tf_op jit(solution)/shard_map/slice | solution.py:13
  707.9 305.5 %slice_reduce_fusion.1 = bf16[8,924,1024]{2,1,0:T(8,128)(2,1)} fusion(bf16[2,8,924,1024]{3,0,2,1:T(2,128)(2,1)} %bitcast.158), kind=kLoop, calls=%fused_computation.6 | loop fusion | bytes 30277632 | tf_op jit(solution)/shard_map/slice | solution.py:13
  1013.4 11.4 squeeze.26
  1024.8 11.6 squeeze.24
  1036.3 7.8 fusion.43
  1052.4 9.5 pad_maximum_fusion
  1061.9 11.9 copy.109
  1073.9 200.5 %all-reduce.8.cloned.1.call-done = f32[7392,2,256]{2,0,1:T(8,128)} async-done(((f32[7392,2,256]{2,0,1:T(8,128)}), f32[7392,2,256]{2,0,1:T(8,128)}) %all-reduce.8.cloned.1.call-update) | async-done | bytes 15138832 | tf_op jit(solution)/shard_map/psum | solution.py:61
  1274.4 31.0 %fusion.61 = f32[2,256,256]{1,2,0:T(8,128)} fusion(f32[7392,2,256]{2,0,1:T(8,128)} %all-reduce.8.cloned.1.call-done), kind=kOutput, calls=%fused_computation.107 | convolution fusion | flops 11626610688 | bytes 15663104 | tf_op jit(solution)/shard_map/rmk,rml->mkl/dot_general | solution.py:20
  1305.5 38.6 %all-reduce.10.cloned.1.call-done = f32[2,256,256]{1,2,0:T(8,128)} async-done(((f32[2,256,256]{1,2,0:T(8,128)}), f32[2,256,256]{1,2,0:T(8,128)}) %all-reduce.10.cloned.1.call-update) | async-done | bytes 524304 | tf_op jit(solution)/shard_map/psum | solution.py:62
  1346.5 23.5 %custom-call.17 = f32[2,128,128]{2,1,0:T(8,128)S(1)} custom-call(f32[2,128,128]{2,1,0:T(8,128)S(1)} %cholesky.198), custom_call_target="Cholesky" | custom-call | tf_op jit(solution)/shard_map/jit(cholesky)/cholesky | solution.py:24
  1370.0 19.7 custom-call.18
  1390.4 23.5 %custom-call.19 = f32[2,128,128]{2,1,0:T(8,128)S(1)} custom-call(f32[2,128,128]{2,1,0:T(8,128)S(1)} %convolution_subtract_fusion.3), custom_call_target="Cholesky" | custom-call | tf_op jit(solution)/shard_map/jit(cholesky)/cholesky | solution.py:24
  1418.1 39.3 %custom-call.20 = f32[2,2,128,128]{2,3,1,0:T(8,128)S(1)} custom-call(f32[2,2,128,128]{3,2,1,0:T(8,128)S(1)} %bitcast.175), custom_call_target="InvertDiagBlocksLowerTriangular" | custom-call | tf_op jit(solution)/shard_map/jit(_solve_triangular)/vmap()/triangular_solve | solution.py:26
  1457.5 8.9 fusion.3
  1466.4 6.7 convolution_subtract_fusion.1
  1473.1 7.5 fusion.54
  1480.6 8.3 fusion
  1488.9 10.2 copy.71
  1499.1 8.9 fusion.21
  1517.7 43.5 %reduce-scatter.2.cloned.1.call-done = f32[2,256,256]{2,1,0:T(8,128)} async-done(((f32[2,1024,256]{2,1,0:T(8,128)}), f32[2,256,256]{2,1,0:T(8,128)}) %reduce-scatter.2.cloned.1.call-update) | async-done | bytes 524304 | tf_op jit(solution)/shard_map/reduce_scatter | solution.py:69
  1563.1 27.4 %all-gather.2.cloned.1.call-done = bf16[2,1024,256]{2,1,0:T(8,128)(2,1)} async-done(((bf16[2,256,256]{2,1,0:T(8,128)(2,1)}), bf16[2,1024,256]{2,1,0:T(8,128)(2,1)}) %all-gather.2.cloned.1.call-update) | async-done | bytes 1048592 | tf_op jit(solution)/shard_map/all_gather | solution.py:70
  1590.4 9.8 fusion.40
  1600.3 7.6 fusion.39
  1613.8 11.9 copy.108
  1625.7 199.8 %all-reduce.12.cloned.1.call-done = f32[7392,2,256]{2,0,1:T(8,128)} async-done(((f32[7392,2,256]{2,0,1:T(8,128)}), f32[7392,2,256]{2,0,1:T(8,128)}) %all-reduce.12.cloned.1.call-update) | async-done | bytes 15138832 | tf_op jit(solution)/shard_map/psum | solution.py:61
  1825.6 30.9 %fusion.62 = f32[2,256,256]{1,2,0:T(8,128)} fusion(f32[7392,2,256]{2,0,1:T(8,128)} %all-reduce.12.cloned.1.call-done), kind=kOutput, calls=%fused_computation.108 | convolution fusion | flops 11626610688 | bytes 15663104 | tf_op jit(solution)/shard_map/rmk,rml->mkl/dot_general | solution.py:20
  1856.5 38.7 %all-reduce.14.cloned.1.call-done = f32[2,256,256]{1,2,0:T(8,128)} async-done(((f32[2,256,256]{1,2,0:T(8,128)}), f32[2,256,256]{1,2,0:T(8,128)}) %all-reduce.14.cloned.1.call-update) | async-done | bytes 524304 | tf_op jit(solution)/shard_map/psum | solution.py:62
  1897.6 23.5 %custom-call.21 = f32[2,128,128]{2,1,0:T(8,128)S(1)} custom-call(f32[2,128,128]{2,1,0:T(8,128)S(1)} %cholesky.201), custom_call_target="Cholesky" | custom-call | tf_op jit(solution)/shard_map/jit(cholesky)/cholesky | solution.py:24
  1921.1 19.7 custom-call.22
  1941.5 23.5 %custom-call.23 = f32[2,128,128]{2,1,0:T(8,128)S(1)} custom-call(f32[2,128,128]{2,1,0:T(8,128)S(1)} %convolution_subtract_fusion.2), custom_call_target="Cholesky" | custom-call | tf_op jit(solution)/shard_map/jit(cholesky)/cholesky | solution.py:24
  1969.3 39.3 %custom-call.24 = f32[2,2,128,128]{2,3,1,0:T(8,128)S(1)} custom-call(f32[2,2,128,128]{3,2,1,0:T(8,128)S(1)} %bitcast.174), custom_call_target="InvertDiagBlocksLowerTriangular" | custom-call | tf_op jit(solution)/shard_map/jit(_solve_triangular)/vmap()/triangular_solve | solution.py:26
  2008.6 8.9 fusion.1
  2017.5 6.7 convolution_subtract_fusion
  2024.2 8.2 fusion.50
  2032.3 11.6 maximum_bitcast_fusion
  2044.0 15.4 copy.80
  2059.4 9.1 bitcast_convert_fusion
  2068.5 10.7 fusion.36
  2079.2 7.8 fusion.33
  2095.1 46.1 %all-reduce.16.cloned.1.call-done = bf16[2,1024,256]{1,0,2:T(2,128)(2,1)} async-done(((bf16[2,1024,256]{1,0,2:T(2,128)(2,1)}), bf16[2,1024,256]{1,0,2:T(2,128)(2,1)}) %all-reduce.16.cloned.1.call-update) | async-done | bytes 1048592
  (102 shorter events, 77.5 us)
Async XLA Ops:
  7.2 1267.2 %all-reduce.8.cloned.1.call-start = ((), (), s32[]{:S(2)}) async-start(), calls=%async_computation.2 | async-start | bytes 30277632 | tf_op jit(solution)/shard_map/psum | solution.py:61
  1024.8 11.6 copy-start.7
  1036.3 9.6 copy-start.4
  1073.8 270.3 %all-reduce.10.cloned.1.call-start = ((), (), s32[]{:S(2)}) async-start(), calls=%async_computation.3 | async-start | bytes 1048576 | tf_op jit(solution)/shard_map/psum | solution.py:62
  1305.4 255.8 %reduce-scatter.2.cloned.1.call-start = ((), (), s32[]{:S(2)}) async-start(), calls=%async_computation.4 | async-start | bytes 2621440 | tf_op jit(solution)/shard_map/reduce_scatter | solution.py:69
  1457.5 8.9 copy-start
  1466.4 6.7 copy-start.2
  1499.1 9.0 slice-start
  1499.1 9.8 copy-start.6
  1499.1 11.0 slice-start.1
  1499.1 12.2 slice-start.2
  1499.1 12.9 slice-start.3
  1517.7 72.8 %all-gather.2.cloned.1.call-start = ((), (), s32[]{:S(2)}) async-start(), calls=%async_computation.5 | async-start | bytes 1310720 | tf_op jit(solution)/shard_map/all_gather | solution.py:70
  1563.0 262.5 %all-reduce.12.cloned.1.call-start = ((), (), s32[]{:S(2)}) async-start(), calls=%async_computation.6 | async-start | bytes 30277632 | tf_op jit(solution)/shard_map/psum | solution.py:61
  1590.4 9.8 copy-start.8
  1625.7 269.5 %all-reduce.14.cloned.1.call-start = ((), (), s32[]{:S(2)}) async-start(), calls=%async_computation.7 | async-start | bytes 1048576 | tf_op jit(solution)/shard_map/psum | solution.py:62
  1856.5 284.7 %all-reduce.16.cloned.1.call-start = ((), (), s32[]{:S(2)}) async-start(), calls=%async_computation.8 | async-start | bytes 2097152
  2008.6 8.9 copy-start.1
  2017.5 6.7 copy-start.3
  2068.5 10.7 copy-start.5
  2079.2 10.2 copy-start.9
Sparse Core Ops, SparseCore 0:
  1073.9 200.4 all-reduce.7
  1305.5 38.5 all-reduce.9
  1517.8 43.3 reduce-scatter.1
  1563.2 27.1 all-gather.1
  1625.8 199.7 all-reduce.11
  1856.6 38.5 all-reduce.13
  2089.5 51.7 all-reduce.15
